TPU v7x, 32 devices: a whole 2x2x4 slice. The times are simulated.
32 devices in a mesh: section: 2 (over x), view: 8 (over z, y), scene: 2 (over core).
Axes of the slice: x: 2, y: 2, z: 4, core: 2. Of those that a mesh axis runs over, the one named last changes fastest.
Arguments:
- tokens: bfloat16 [2, 512, 1024], P('scene', ('section', 'view')), may hold values from -6 to 6
- norm_gain: float32 [1024], replicated, may hold values from 0.1 to 1.9
- head_weight: bfloat16 [1024, 512], replicated, may hold values from -0.1875 to 0.1875
- tile_lists: int32 [2, 64, 128], P('scene', ('section', 'view')), may hold values from 0 to 32767, as said below
- tile_counts: int32 [2, 64], P('scene', ('section', 'view')), may hold values from 1 to 128, as said below
- cameras: float32 [2, 2, 8], P('scene'), may hold values from -3 to 3
- targets: bfloat16 [2, 64, 768], P('scene', ('section', 'view')), may hold values from 0 to 1
Outputs:
- image: bfloat16 [2, 64, 768], P('scene', ('section', 'view'))
- grad_head: float32 [1024, 512], replicated
- loss: float32 [], replicated
Inputs may be any that keep to these rules, and one draw needn't show every extreme that they name: `tile_lists`: gaussian n of a scene has owner n // 2048. Among the 512 slots (live or not) of each aligned block of 4 tiles, at most 64 name Gaussians of one owner, and in every such block some owner is named exactly 64 times. `tile_counts`: the first tile of each scene has 128 live slots.
All inputs are finite; a program needn't handle non-finite values.
Results may differ from a plain program's by a relative error of at most 0.014.
Values may be sent and summed in bfloat16 or wider, within the bound.
A program may use at most 256 MiB of HBM per device.

v0:
```python
import jax
import jax.numpy as jnp
from jax import lax
from jax.sharding import PartitionSpec as P

GPT = 64
PARAMS = 8
K = 128
SIDE = 16
VIEWS = 2


def pixel_grid():
    place = jnp.arange(SIDE * SIDE, dtype=jnp.int32)
    across = ((place % SIDE).astype(jnp.float32) + 0.5) * (2.0 / SIDE) - 1.0
    down = ((place // SIDE).astype(jnp.float32) + 0.5) * (2.0 / SIDE) - 1.0
    return (across, down)


def composite(values, live, cams, wanted, across, down):
    slots = jnp.arange(K, dtype=jnp.int32)
    strict = (slots[:, None] < slots[None, :]).astype(jnp.float32)
    sx = jnp.tanh(
        cams[:, 0:1] * values[0]
        + cams[:, 1:2] * values[1]
        + cams[:, 2:3] * values[2]
        + cams[:, 3:4]
    )
    sy = jnp.tanh(
        cams[:, 4:5] * values[0]
        + cams[:, 5:6] * values[1]
        + cams[:, 6:7] * values[2]
        + cams[:, 7:8]
    )
    spread = jnp.exp(-2.0 * values[3])
    dxx = across[None, None, :] - sx[:, :, None]
    dyy = down[None, None, :] - sy[:, :, None]
    alpha = (
        0.3
        * jax.nn.sigmoid(values[4])[:, :, None]
        * jnp.exp(-0.5 * (dxx * dxx + dyy * dyy) * spread[:, :, None])
        * live[:, :, None]
    )
    logs = jnp.log1p(-alpha)
    before = jnp.einsum("bkp,kj->bjp", logs, strict, precision=lax.Precision.HIGHEST)
    weight = alpha * jnp.exp(before)
    colour = jnp.einsum(
        "bkp,cbk->bcp", weight, jax.nn.sigmoid(values[5:8]), precision=lax.Precision.HIGHEST
    )
    colour = colour.reshape(colour.shape[0], 3 * SIDE * SIDE)
    diff = colour - wanted.astype(jnp.float32)
    return (jnp.sum(diff * diff), colour)


def to_gauss(head, rows):
    return (
        head.reshape(rows, PARAMS, GPT)
        .transpose(1, 0, 2)
        .reshape(PARAMS, rows * GPT)
        .astype(jnp.bfloat16)
    )


def body(tokens, norm_gain, head_weight, tile_lists, tile_counts, cameras, targets):
    tok_rows = tokens.shape[1]
    tile_rows = tile_lists.shape[1]
    group = lax.axis_size(("section", "view"))
    scenes_all = lax.axis_size("scene")
    tiles_all = tile_rows * group
    factor = 1.0 / (scenes_all * tiles_all)
    values_in = tokens[0].astype(jnp.float32)
    scale = lax.rsqrt(jnp.mean(values_in * values_in, axis=-1, keepdims=True) + 1e-06)
    normed = (values_in * scale * norm_gain).astype(jnp.bfloat16)
    lists = tile_lists[0]
    own_count = tok_rows * GPT
    slot_total = tile_rows * K
    bucket = 2 * ((slot_total + group - 1) // group)
    flat = lists.reshape(-1)
    owner = flat // own_count
    inner = flat - owner * own_count
    order = jnp.argsort(owner, stable=True)
    sorted_owner = owner[order]
    owner_ids = jnp.arange(group, dtype=jnp.int32)
    per_owner = jnp.sum((owner[:, None] == owner_ids[None, :]).astype(jnp.int32), axis=0)
    starts = jnp.cumsum(per_owner) - per_owner
    rank = jnp.arange(slot_total, dtype=jnp.int32) - starts[sorted_owner]
    target_slot = jnp.zeros((slot_total,), jnp.int32).at[order].set(sorted_owner * bucket + rank)
    wanted_rows = (
        jnp.zeros((group * bucket,), jnp.int32).at[target_slot].set(inner).reshape(group, bucket)
    )
    asked = lax.all_to_all(
        wanted_rows, ("section", "view"), split_axis=0, concat_axis=0, tiled=True
    )
    head = jnp.dot(normed, head_weight, preferred_element_type=jnp.float32)
    own_gauss = to_gauss(head, tok_rows)
    answer = (
        jnp.take(own_gauss, asked.reshape(-1), axis=1)
        .reshape(PARAMS, group, bucket)
        .transpose(1, 0, 2)
    )
    received = lax.all_to_all(answer, ("section", "view"), split_axis=0, concat_axis=0, tiled=True)
    table = received.transpose(1, 0, 2).reshape(PARAMS, group * bucket).astype(jnp.float32)
    values = jnp.take(table, target_slot, axis=1).reshape(PARAMS, tile_rows, K)
    per_view = tiles_all // VIEWS
    first_tile = lax.axis_index(("section", "view")) * tile_rows
    which = (first_tile + jnp.arange(tile_rows, dtype=jnp.int32)) // per_view
    onehot = (which[:, None] == jnp.arange(VIEWS, dtype=jnp.int32)[None, :]).astype(jnp.float32)
    tile_cams = jnp.dot(onehot, cameras[0], precision=lax.Precision.HIGHEST)
    slots = jnp.arange(K, dtype=jnp.int32)
    live = (slots[None, :] < tile_counts[0][:, None]).astype(jnp.float32)
    across, down = pixel_grid()

    def local(vals):
        return composite(vals, live, tile_cams, targets[0], across, down)

    part, pullback, colour = jax.vjp(local, values, has_aux=True)
    grads = pullback(jnp.ones_like(part) * factor)[0]
    outgoing = (
        jnp.zeros((PARAMS, group * bucket), jnp.float32)
        .at[:, target_slot]
        .set(grads.reshape(PARAMS, -1))
    )
    outgoing = outgoing.reshape(PARAMS, group, bucket).transpose(1, 0, 2)
    returned = lax.all_to_all(
        outgoing.astype(jnp.bfloat16), ("section", "view"), split_axis=0, concat_axis=0, tiled=True
    ).astype(outgoing.dtype)
    own = (
        jnp.zeros((PARAMS, own_count), jnp.float32)
        .at[:, asked.reshape(-1)]
        .add(returned.transpose(1, 0, 2).reshape(PARAMS, -1))
    )
    dhead = own.reshape(PARAMS, tok_rows, GPT).transpose(1, 0, 2).reshape(tok_rows, PARAMS * GPT)
    partial_grad = jnp.dot(normed.astype(jnp.float32).T, dhead, precision=lax.Precision.HIGHEST)
    grad_head, loss = lax.psum((partial_grad, part * factor), ("section", "view", "scene"))
    return (colour.astype(jnp.bfloat16)[None], grad_head, loss)


def solution(mesh):
    in_specs = (
        P("scene", ("section", "view"), None),
        P(),
        P(),
        P("scene", ("section", "view"), None),
        P("scene", ("section", "view")),
        P("scene", None, None),
        P("scene", ("section", "view"), None),
    )
    out_specs = (P("scene", ("section", "view"), None), P(), P())
    return jax.shard_map(body, mesh=mesh, in_specs=in_specs, out_specs=out_specs, check_vma=False)
```

profile of v0, /device:TPU:0, one launch (start us, length us, event | category | flops | bytes accessed | tf_op | source)
XLA Modules:
  0.0 234.9 jit_solution(6555050550553904931)
XLA Ops:
  7.2 0.8 bitcast_subtract_fusion
  8.1 3.8 %sort.17 = (s32[512]{0:T(512)}, s32[512]{0:T(512)S(1)}) sort(s32[512]{0:T(512)S(1)} %get-tuple-element.51, s32[512]{0:T(512)S(1)} %iota.50), dimensions={0}, to_apply=%region_0.0 | sort | flops 4608 | bytes 8192 | tf_op jit(solution)/shard_map/jit(argsort)/sort | solution.py:81
  11.9 3.5 %gather_fusion = s32[512]{0:T(512)S(1)} fusion(s32[512]{0:T(512)S(1)} %get-tuple-element.51, s32[1024]{0:T(1024)S(1)} %pad_clamp_fusion.1), kind=kCustom, calls=%fused_computation | custom fusion | bytes 6144 | tf_op jit(solution)/shard_map/gather | solution.py:82
  16.4 4.3 %compare_select_fusion.3 = (s32[512,1]{0,1:T(1,128)S(1)}, s32[512,1]{0,1:T(1,128)S(1)}) fusion(s32[]{:T(128)} %bitcast.12, s32[]{:T(128)} %bitcast.13, s32[]{:T(128)} %bitcast.14, s32[]{:T(128)} %bitcast.15, s32[]{:T(128)} %bitcast.16, s32[]{:T(128)} %bitcast.18, s32[]{:T(128)} %bitcast.17, s32[512,1]{0,1:T(1,128)S(1)} %bitcast.179), kind=kLoop, calls=%fused_computation.113 | loop fusion | flops 7680 | bytes 6172 | tf_op jit(solution)/shard_map/gather | solution.py:86
  20.8 5.7 %fusion.82 = s32[512]{0:T(512)S(1)} fusion(pred[512]{0:T(512)(128)(4,1)S(1)} %get-tuple-element.25, pred[512]{0:T(512)(128)(4,1)S(1)} %get-tuple-element.24, pred[512]{0:T(512)(128)(4,1)S(1)} %get-tuple-element.23, pred[512]{0:T(512)(128)(4,1)S(1)} %get-tuple-element.22, pred[512]{0:T(512)(128)(4,1)S(1)} %get-tuple-element.21, ...), kind=kLoop, calls=%fused_computation.148 | loop fusion | flops 6144 | bytes 10788 | tf_op jit(solution)/shard_map/add | solution.py:87
  26.5 2.4 %scatter_custom_fusion = s32[512]{0:T(512)S(1)} fusion(s32[512]{0:T(512)S(1)} %compare_select_fusion.10, s32[512]{0:T(512)S(1)} %fusion.82, s32[]{:T(128)} %constant.112.clone.1), kind=kCustom, calls=%fused_computation.196 | custom fusion | bytes 2052 | tf_op jit(solution)/shard_map/scatter | solution.py:87
  29.0 2.4 %scatter_custom_fusion.1 = s32[1024]{0:T(1024)S(1)} fusion(s32[512]{0:T(512)S(1)} %compare_select_fusion.9, s32[512]{0:T(512)S(1)} %get-tuple-element.50, s32[]{:T(128)} %constant.112.clone.1), kind=kCustom, calls=%fused_computation.162 | custom fusion | bytes 4100 | tf_op jit(solution)/shard_map/scatter | solution.py:89
  32.1 8.3 %all-to-all-start = ((s32[16,1,64]{2,1,0:T(1,128)}), s32[16,1,64]{2,1,0:T(1,128)S(1)}, u32[]{:S(2)}, u32[]{:S(2)}) async-start(s32[16,1,64]{2,1,0:T(1,128)} %all_to_all.12), calls=%async_computation | async-start | bytes 16384 | tf_op jit(solution)/shard_map/all_to_all | solution.py:91
  42.8 4.9 %all-to-all-done = s32[16,1,64]{2,1,0:T(1,128)S(1)} async-done(((s32[16,1,64]{2,1,0:T(1,128)}), s32[16,1,64]{2,1,0:T(1,128)S(1)}, u32[]{:S(2)}, u32[]{:S(2)}) %all-to-all-start) | async-done | bytes 4128 | tf_op jit(solution)/shard_map/all_to_all | solution.py:91
  49.0 3.2 %gather_fusion.1 = bf16[1024,8]{1,0:T(8,128)(2,1)S(1)} fusion(bf16[8,2048]{0,1:T(8,128)(2,1)S(1)} %bitcast.162, s32[1024]{0:T(1024)S(1)} %broadcast_clamp_fusion), kind=kCustom, calls=%fused_computation.1 | custom fusion | bytes 36864 | tf_op jit(solution)/shard_map/jit(_take)/gather | solution.py:97
  53.1 3.5 %all-to-all-start.1 = ((bf16[16,2,256]{2,1,0:T(2,128)(2,1)}), bf16[16,2,256]{2,1,0:T(2,128)(2,1)S(1)}, u32[]{:S(2)}, u32[]{:S(2)}) async-start(bf16[16,2,256]{2,1,0:T(2,128)(2,1)} %reshape.1807), calls=%async_computation.1 | async-start | bytes 32768 | tf_op jit(solution)/shard_map/all_to_all | solution.py:101
  56.7 7.2 %all-to-all-done.1 = bf16[16,2,256]{2,1,0:T(2,128)(2,1)S(1)} async-done(((bf16[16,2,256]{2,1,0:T(2,128)(2,1)}), bf16[16,2,256]{2,1,0:T(2,128)(2,1)S(1)}, u32[]{:S(2)}, u32[]{:S(2)}) %all-to-all-start.1) | async-done | bytes 16416 | tf_op jit(solution)/shard_map/all_to_all | solution.py:101
  64.2 1.0 gather_fusion.2
  65.5 0.9 convolution_exponential_fusion
  66.4 1.3 multiply_reduce_fusion
  67.7 0.9 fusion.52
  69.3 1.6 fusion.19
  71.3 1.8 scatter_custom_fusion.2
  73.4 9.9 %all_to_all.19 = bf16[16,2,256]{2,1,0:T(2,128)(2,1)S(1)} all-to-all(bf16[16,2,256]{2,1,0:T(2,128)(2,1)S(1)} %reshape.1809), channel_id=1, replica_groups=mesh['section'=2,'view'=8,'scene'=2] {'section','view'}, dimensions={0} | all-to-all | bytes 32768 | tf_op jit(solution)/shard_map/all_to_all | solution.py:124
  83.7 6.7 %scatter_custom_fusion.3 = f32[8,2048]{0,1:T(8,128)S(1)} fusion(s32[1024]{0:T(1024)S(1)} %bitcast.181, f32[1024,8]{1,0:T(8,128)S(1)} %copy.137, f32[]{:T(128)} %constant.123.clone.1), kind=kCustom, calls=%fused_computation.48 | custom fusion | flops 8192 | bytes 65540 | tf_op jit(solution)/shard_map/scatter-add | solution.py:130
  90.9 2.4 %fusion.58 = f32[1024,512]{1,0:T(8,128)} fusion(f32[32,512]{1,0:T(8,128)S(1)} %reshape.1631, bf16[1,32,1024]{2,1,0:T(8,128)(2,1)S(1)} %copy-done.2, f32[1024]{0:T(1024)S(1)} %copy-done.3, f32[32]{0:T(128)S(1)} %add_rsqrt_fusion), kind=kOutput, calls=%fused_computation.76 | convolution fusion | flops 201457664 | bytes 2232448 | tf_op jit(solution)/shard_map/dot_general | solution.py:133
  93.9 38.3 %psum.15 = f32[]{:T(128)} all-reduce(f32[]{:T(128)S(6)} %mul.699), channel_id=1, replica_groups=mesh['section'=2,'view'=8,'scene'=2] {'section','view','scene'}, use_global_device_ids=true, to_apply=%region_14.15 | all-reduce | flops 1 | bytes 8 | tf_op jit(solution)/shard_map/psum | solution.py:134
  132.9 92.1 %all-reduce.11.cloned.1.call-done = f32[1024,512]{1,0:T(8,128)} async-done(((f32[1024,512]{1,0:T(8,128)}), f32[1024,512]{1,0:T(8,128)}) %all-reduce.11.cloned.1.call-update) | async-done | bytes 2097168 | tf_op jit(solution)/shard_map/psum | solution.py:134
  225.0 3.1 %copy.158 = f32[1024,512]{1,0:T(8,128)} copy(f32[1024,512]{1,0:T(8,128)} %all-reduce.11.cloned.1.call-done) | data formatting | bytes 4194304
  (79 shorter events, 9.5 us)
Async XLA Ops:
  7.2 33.6 %copy-start = (f32[1,2,8]{2,1,0:T(2,128)S(1)}, f32[1,2,8]{2,1,0:T(2,128)}, u32[]{:S(2)}) copy-start(f32[1,2,8]{2,1,0:T(2,128)} %param.12) | copy-start | bytes 196
  7.2 33.3 %copy-start.5 = (s32[1,4]{1,0:T(1,128)S(1)}, s32[1,4]{1,0:T(1,128)}, u32[]{:S(2)}) copy-start(s32[1,4]{1,0:T(1,128)} %param.11) | copy-start | bytes 52
  7.2 33.5 %copy-start.2 = (bf16[1,32,1024]{2,1,0:T(8,128)(2,1)S(1)}, bf16[1,32,1024]{2,1,0:T(8,128)(2,1)}, u32[]{:S(2)}) copy-start(bf16[1,32,1024]{2,1,0:T(8,128)(2,1)} %param.7) | copy-start | bytes 196612
  7.2 34.1 %copy-start.1 = (bf16[1024,512]{1,0:T(8,128)(2,1)S(1)}, bf16[1024,512]{1,0:T(8,128)(2,1)}, u32[]{:S(2)}) copy-start(bf16[1024,512]{1,0:T(8,128)(2,1)} %param.9) | copy-start | bytes 3145732
  11.9 30.0 %copy-start.3 = (f32[1024]{0:T(1024)S(1)}, f32[1024]{0:T(1024)}, u32[]{:S(2)}) copy-start(f32[1024]{0:T(1024)} %param.8) | copy-start | bytes 12292
  32.1 15.6 %all-to-all-start = ((s32[16,1,64]{2,1,0:T(1,128)}), s32[16,1,64]{2,1,0:T(1,128)S(1)}, u32[]{:S(2)}, u32[]{:S(2)}) async-start(s32[16,1,64]{2,1,0:T(1,128)} %all_to_all.12), calls=%async_computation | async-start | bytes 16384 | tf_op jit(solution)/shard_map/all_to_all | solution.py:91
  41.3 15.3 %copy-start.4 = (bf16[1,4,768]{2,1,0:T(4,128)(2,1)S(1)}, bf16[1,4,768]{2,1,0:T(4,128)(2,1)}, u32[]{:S(2)}) copy-start(bf16[1,4,768]{2,1,0:T(4,128)(2,1)} %param.13) | copy-start | bytes 18436
  53.1 10.8 %all-to-all-start.1 = ((bf16[16,2,256]{2,1,0:T(2,128)(2,1)}), bf16[16,2,256]{2,1,0:T(2,128)(2,1)S(1)}, u32[]{:S(2)}, u32[]{:S(2)}) async-start(bf16[16,2,256]{2,1,0:T(2,128)(2,1)} %reshape.1807), calls=%async_computation.1 | async-start | bytes 32768 | tf_op jit(solution)/shard_map/all_to_all | solution.py:101
  56.6 168.4 %all-reduce.11.cloned.1.call-start = ((), (), s32[]{:S(2)}) async-start(), calls=%async_computation.3 | async-start | bytes 4194304 | tf_op jit(solution)/shard_map/psum | solution.py:134
Sparse Core Ops, SparseCore 0:
  93.4 131.5 all-reduce.10
where the time goes:
time: 236 us; the launch traced here: 235 us
  waiting for transfers between devices  104 us (44%)
  blocking collectives  48.3 us (20%)
  local copies, waits for them, and re-layouts  23.8 us (10%)
  other arithmetic  23.1 us (10%)
  between operations  15.1 us (6%)
  starting transfers between devices  11.9 us (5%)
  matrix products  8.56 us (4%)
    psum x1, waiting for transfers between devices, body(): lax.psum((partial_grad, part * factor), ('section', 'view', 'scene'))  92.1 us
    psum x1, blocking collectives, body(): lax.psum((partial_grad, part * factor), ('section', 'view', 'scene'))  38.3 us
    all_to_all x1, blocking collectives, body(): lax.all_to_all(outgoing.astype(jnp.bfloat16), ('section', 'view'), split_...  9.91 us
    all_to_all x1, starting transfers between devices, body(): lax.all_to_all(wanted_rows, ('section', 'view'), split_axis=0, concat_axi...  8.34 us
    all_to_all x1, waiting for transfers between devices, body(): lax.all_to_all(answer, ('section', 'view'), split_axis=0, concat_axis=0,...  7.22 us
    scatter-add x1, other arithmetic, body(): own = jnp.zeros((PARAMS, own_count), jnp.float32).at[:, asked.reshape(-1)...  6.72 us
    add x1, other arithmetic, body(): sorted_owner * bucket + rank  5.71 us
    all_to_all x1, waiting for transfers between devices, body(): lax.all_to_all(wanted_rows, ('section', 'view'), split_axis=0, concat_axi...  4.9 us
  transfers between devices with their start and end apart: 3, of which 3 were waited for; matrix products, arithmetic and copies ran while one was open for 1% of the time, Pallas kernels for 0%

commit v1 on v0

--- a/solution.py
+++ b/solution.py
@@ -131,7 +131,9 @@
     )
     dhead = own.reshape(PARAMS, tok_rows, GPT).transpose(1, 0, 2).reshape(tok_rows, PARAMS * GPT)
     partial_grad = jnp.dot(normed.astype(jnp.float32).T, dhead, precision=lax.Precision.HIGHEST)
-    grad_head, loss = lax.psum((partial_grad, part * factor), ("section", "view", "scene"))
+    grad_head, loss = lax.psum(
+        lax.psum((partial_grad, part * factor), ("view", "scene")), "section"
+    )
     return (colour.astype(jnp.bfloat16)[None], grad_head, loss)
 
 

time: 236 us -> 263 us (1.11)
  waiting for transfers between devices: 104 us -> 134 us
    psum x1 -> x2, waiting for transfers between devices: 92.1 us -> 122 us  [the longest x1 94.7 us: body(): lax.psum((partial_grad, part * factor), ('view', 'scene'))]
    psum x1 -> x2, blocking collectives: 38.3 us -> 36.4 us  [the longest x1 30.9 us: body(): lax.psum((partial_grad, part * factor), ('view', 'scene'))]
  transfers between devices with their start and end apart: 3 -> 4, of which waited for: 3 -> 4; matrix products, arithmetic and copies ran while one was open for 1% -> 1% of each run, Pallas kernels for 0% -> 0%
where the time goes in v1:
time: 263 us
  waiting for transfers between devices  134 us (51%)
  blocking collectives  46.3 us (18%)
  local copies, waits for them, and re-layouts  23.8 us (9%)
  other arithmetic  23.1 us (9%)
  between operations  15.1 us (6%)
  starting transfers between devices  11.9 us (5%)
  matrix products  8.56 us (3%)
    psum x1, waiting for transfers between devices, body(): lax.psum((partial_grad, part * factor), ('view', 'scene'))  94.7 us
    psum x1, blocking collectives, body(): lax.psum((partial_grad, part * factor), ('view', 'scene'))  30.9 us
    psum x1, waiting for transfers between devices, body(): lax.psum(lax.psum((partial_grad, part * factor), ('view', 'scene')), 'sec...  26.9 us
    all_to_all x1, blocking collectives, body(): lax.all_to_all(outgoing.astype(jnp.bfloat16), ('section', 'view'), split_...  9.91 us
    all_to_all x1, starting transfers between devices, body(): lax.all_to_all(wanted_rows, ('section', 'view'), split_axis=0, concat_axi...  8.34 us
    all_to_all x1, waiting for transfers between devices, body(): lax.all_to_all(answer, ('section', 'view'), split_axis=0, concat_axis=0,...  7.22 us
    scatter-add x1, other arithmetic, body(): own = jnp.zeros((PARAMS, own_count), jnp.float32).at[:, asked.reshape(-1)...  6.72 us
    add x1, other arithmetic, body(): sorted_owner * bucket + rank  5.71 us
  transfers between devices with their start and end apart: 4, of which 4 were waited for; matrix products, arithmetic and copies ran while one was open for 1% of the time, Pallas kernels for 0%

profile of v1, /device:TPU:0, one launch (start us, length us, event | category | flops | bytes accessed | tf_op | source)
XLA Modules:
  0.0 262.6 jit_solution(14201487273805411756)
XLA Ops:
  8.1 3.8 %sort.17 = (s32[512]{0:T(512)}, s32[512]{0:T(512)S(1)}) sort(s32[512]{0:T(512)S(1)} %get-tuple-element.51, s32[512]{0:T(512)S(1)} %iota.50), dimensions={0}, to_apply=%region_0.0 | sort | flops 4608 | bytes 8192 | tf_op jit(solution)/shard_map/jit(argsort)/sort | solution.py:81
  11.9 3.5 %gather_fusion = s32[512]{0:T(512)S(1)} fusion(s32[512]{0:T(512)S(1)} %get-tuple-element.51, s32[1024]{0:T(1024)S(1)} %pad_clamp_fusion.1), kind=kCustom, calls=%fused_computation | custom fusion | bytes 6144 | tf_op jit(solution)/shard_map/gather | solution.py:82
  16.4 4.3 %compare_select_fusion.3 = (s32[512,1]{0,1:T(1,128)S(1)}, s32[512,1]{0,1:T(1,128)S(1)}) fusion(s32[]{:T(128)} %bitcast.12, s32[]{:T(128)} %bitcast.13, s32[]{:T(128)} %bitcast.14, s32[]{:T(128)} %bitcast.15, s32[]{:T(128)} %bitcast.16, s32[]{:T(128)} %bitcast.18, s32[]{:T(128)} %bitcast.17, s32[512,1]{0,1:T(1,128)S(1)} %bitcast.179), kind=kLoop, calls=%fused_computation.113 | loop fusion | flops 7680 | bytes 6172 | tf_op jit(solution)/shard_map/gather | solution.py:86
  20.8 5.7 %fusion.82 = s32[512]{0:T(512)S(1)} fusion(pred[512]{0:T(512)(128)(4,1)S(1)} %get-tuple-element.25, pred[512]{0:T(512)(128)(4,1)S(1)} %get-tuple-element.24, pred[512]{0:T(512)(128)(4,1)S(1)} %get-tuple-element.23, pred[512]{0:T(512)(128)(4,1)S(1)} %get-tuple-element.22, pred[512]{0:T(512)(128)(4,1)S(1)} %get-tuple-element.21, ...), kind=kLoop, calls=%fused_computation.148 | loop fusion | flops 6144 | bytes 10788 | tf_op jit(solution)/shard_map/add | solution.py:87
  26.5 2.4 scatter_custom_fusion
  29.0 2.4 scatter_custom_fusion.1
  32.1 8.3 %all-to-all-start = ((s32[16,1,64]{2,1,0:T(1,128)}), s32[16,1,64]{2,1,0:T(1,128)S(1)}, u32[]{:S(2)}, u32[]{:S(2)}) async-start(s32[16,1,64]{2,1,0:T(1,128)} %all_to_all.12), calls=%async_computation | async-start | bytes 16384 | tf_op jit(solution)/shard_map/all_to_all | solution.py:91
  42.8 4.9 %all-to-all-done = s32[16,1,64]{2,1,0:T(1,128)S(1)} async-done(((s32[16,1,64]{2,1,0:T(1,128)}), s32[16,1,64]{2,1,0:T(1,128)S(1)}, u32[]{:S(2)}, u32[]{:S(2)}) %all-to-all-start) | async-done | bytes 4128 | tf_op jit(solution)/shard_map/all_to_all | solution.py:91
  49.0 3.2 %gather_fusion.1 = bf16[1024,8]{1,0:T(8,128)(2,1)S(1)} fusion(bf16[8,2048]{0,1:T(8,128)(2,1)S(1)} %bitcast.162, s32[1024]{0:T(1024)S(1)} %broadcast_clamp_fusion), kind=kCustom, calls=%fused_computation.1 | custom fusion | bytes 36864 | tf_op jit(solution)/shard_map/jit(_take)/gather | solution.py:97
  53.1 3.5 %all-to-all-start.1 = ((bf16[16,2,256]{2,1,0:T(2,128)(2,1)}), bf16[16,2,256]{2,1,0:T(2,128)(2,1)S(1)}, u32[]{:S(2)}, u32[]{:S(2)}) async-start(bf16[16,2,256]{2,1,0:T(2,128)(2,1)} %reshape.1807), calls=%async_computation.1 | async-start | bytes 32768 | tf_op jit(solution)/shard_map/all_to_all | solution.py:101
  56.7 7.2 %all-to-all-done.1 = bf16[16,2,256]{2,1,0:T(2,128)(2,1)S(1)} async-done(((bf16[16,2,256]{2,1,0:T(2,128)(2,1)}), bf16[16,2,256]{2,1,0:T(2,128)(2,1)S(1)}, u32[]{:S(2)}, u32[]{:S(2)}) %all-to-all-start.1) | async-done | bytes 16416 | tf_op jit(solution)/shard_map/all_to_all | solution.py:101
  64.2 1.0 gather_fusion.2
  65.5 0.9 convolution_exponential_fusion
  66.4 1.3 multiply_reduce_fusion
  69.3 1.6 fusion.19
  71.3 1.8 scatter_custom_fusion.2
  73.4 9.9 %all_to_all.19 = bf16[16,2,256]{2,1,0:T(2,128)(2,1)S(1)} all-to-all(bf16[16,2,256]{2,1,0:T(2,128)(2,1)S(1)} %reshape.1809), channel_id=1, replica_groups=mesh['section'=2,'view'=8,'scene'=2] {'section','view'}, dimensions={0} | all-to-all | bytes 32768 | tf_op jit(solution)/shard_map/all_to_all | solution.py:124
  83.7 6.7 %scatter_custom_fusion.3 = f32[8,2048]{0,1:T(8,128)S(1)} fusion(s32[1024]{0:T(1024)S(1)} %bitcast.181, f32[1024,8]{1,0:T(8,128)S(1)} %copy.137, f32[]{:T(128)} %constant.123.clone.1), kind=kCustom, calls=%fused_computation.48 | custom fusion | flops 8192 | bytes 65540 | tf_op jit(solution)/shard_map/scatter-add | solution.py:130
  90.9 2.4 fusion.58
  93.3 94.7 %all-reduce.12.cloned.1.call-done = f32[1024,512]{1,0:T(8,128)} async-done(((f32[1024,512]{1,0:T(8,128)}), f32[1024,512]{1,0:T(8,128)}) %all-reduce.12.cloned.1.call-update) | async-done | bytes 2097168 | tf_op jit(solution)/shard_map/psum | solution.py:135
  188.7 30.9 %psum.30 = f32[]{:T(128)} all-reduce(f32[]{:T(128)S(6)} %mul.699), channel_id=1, replica_groups=mesh['section'=2,'view'=8,'scene'=2] {'view','scene'}, use_global_device_ids=true, to_apply=%region_15.16 | all-reduce | flops 1 | bytes 8 | tf_op jit(solution)/shard_map/psum | solution.py:135
  219.6 5.5 %psum.31 = f32[]{:T(128)} all-reduce(f32[]{:T(128)} %psum.30), channel_id=1, replica_groups=mesh['section'=2,'view'=8,'scene'=2] {'section'}, use_global_device_ids=true, to_apply=%region_16.17 | all-reduce | flops 1 | bytes 8 | tf_op jit(solution)/shard_map/psum | solution.py:134
  225.7 26.9 %all-reduce.14.cloned.1.call-done = f32[1024,512]{1,0:T(8,128)} async-done(((f32[1024,512]{1,0:T(8,128)}), f32[1024,512]{1,0:T(8,128)}) %all-reduce.14.cloned.1.call-update) | async-done | bytes 2097168 | tf_op jit(solution)/shard_map/psum | solution.py:134
  252.7 3.1 %copy.159 = f32[1024,512]{1,0:T(8,128)} copy(f32[1024,512]{1,0:T(8,128)} %all-reduce.14.cloned.1.call-done) | data formatting | bytes 4194304
  (83 shorter events, 11.2 us)
Async XLA Ops:
  7.2 33.6 %copy-start = (f32[1,2,8]{2,1,0:T(2,128)S(1)}, f32[1,2,8]{2,1,0:T(2,128)}, u32[]{:S(2)}) copy-start(f32[1,2,8]{2,1,0:T(2,128)} %param.12) | copy-start | bytes 196
  7.2 33.3 %copy-start.5 = (s32[1,4]{1,0:T(1,128)S(1)}, s32[1,4]{1,0:T(1,128)}, u32[]{:S(2)}) copy-start(s32[1,4]{1,0:T(1,128)} %param.11) | copy-start | bytes 52
  7.2 33.5 %copy-start.2 = (bf16[1,32,1024]{2,1,0:T(8,128)(2,1)S(1)}, bf16[1,32,1024]{2,1,0:T(8,128)(2,1)}, u32[]{:S(2)}) copy-start(bf16[1,32,1024]{2,1,0:T(8,128)(2,1)} %param.7) | copy-start | bytes 196612
  7.2 34.1 %copy-start.1 = (bf16[1024,512]{1,0:T(8,128)(2,1)S(1)}, bf16[1024,512]{1,0:T(8,128)(2,1)}, u32[]{:S(2)}) copy-start(bf16[1024,512]{1,0:T(8,128)(2,1)} %param.9) | copy-start | bytes 3145732
  11.9 30.0 %copy-start.3 = (f32[1024]{0:T(1024)S(1)}, f32[1024]{0:T(1024)}, u32[]{:S(2)}) copy-start(f32[1024]{0:T(1024)} %param.8) | copy-start | bytes 12292
  32.1 15.6 %all-to-all-start = ((s32[16,1,64]{2,1,0:T(1,128)}), s32[16,1,64]{2,1,0:T(1,128)S(1)}, u32[]{:S(2)}, u32[]{:S(2)}) async-start(s32[16,1,64]{2,1,0:T(1,128)} %all_to_all.12), calls=%async_computation | async-start | bytes 16384 | tf_op jit(solution)/shard_map/all_to_all | solution.py:91
  41.3 15.3 %copy-start.4 = (bf16[1,4,768]{2,1,0:T(4,128)(2,1)S(1)}, bf16[1,4,768]{2,1,0:T(4,128)(2,1)}, u32[]{:S(2)}) copy-start(bf16[1,4,768]{2,1,0:T(4,128)(2,1)} %param.13) | copy-start | bytes 18436
  53.1 10.8 %all-to-all-start.1 = ((bf16[16,2,256]{2,1,0:T(2,128)(2,1)}), bf16[16,2,256]{2,1,0:T(2,128)(2,1)S(1)}, u32[]{:S(2)}, u32[]{:S(2)}) async-start(bf16[16,2,256]{2,1,0:T(2,128)(2,1)} %reshape.1807), calls=%async_computation.1 | async-start | bytes 32768 | tf_op jit(solution)/shard_map/all_to_all | solution.py:101
  56.6 131.4 %all-reduce.12.cloned.1.call-start = ((), (), s32[]{:S(2)}) async-start(), calls=%async_computation.3 | async-start | bytes 4194304 | tf_op jit(solution)/shard_map/psum | solution.py:135
  93.3 159.4 %all-reduce.14.cloned.1.call-start = ((), (), s32[]{:S(2)}) async-start(), calls=%async_computation.4 | async-start | bytes 4194304 | tf_op jit(solution)/shard_map/psum | solution.py:134
Sparse Core Ops, SparseCore 0:
  93.4 94.5 all-reduce.11
  190.3 62.3 all-reduce.13
